TPU v7x, 128 devices: a whole 4x4x4 slice. The times are simulated.
128 devices in a mesh: cuts: 8 (over y, core), fsdp: 16 (over z, x).
Axes of the slice: x: 4, y: 4, z: 4, core: 2. Of those that a mesh axis runs over, the one named last changes fastest.
Arguments:
- hidden_states: bfloat16 [65536, 8192], P(('cuts', 'fsdp')), may hold values from -1200 to 1200
- key_cotangent: bfloat16 [65536, 512], P(('cuts', 'fsdp')), may hold values from -60 to 60
- old_weight: bfloat16 [16384, 256], P(('cuts', 'fsdp')), may hold values from -0.0625 to 0.0625
- old_first: bfloat16 [16384, 256], P(('cuts', 'fsdp')), may hold values from -1 to 1
- old_first_scale: float32 [16384], P(('cuts', 'fsdp')), may hold values from 3e-05 to 0.0003
- old_second: bfloat16 [16384, 256], P(('cuts', 'fsdp')), may hold values from 0 to 1
- old_second_scale: float32 [16384], P(('cuts', 'fsdp')), may hold values from 1e-08 to 1e-07
- send_counts: int32 [128, 128], P(('cuts', 'fsdp')), may hold values from 0 to 2, as said below
Outputs:
- input_grad: bfloat16 [65536, 8192], P(('cuts', 'fsdp'))
- new_weight: bfloat16 [8192, 512], P(('cuts', 'fsdp'))
- first_code: bfloat16 [8192, 512], P(('cuts', 'fsdp'))
- first_scale: float32 [8192, 2], P(('cuts', 'fsdp'))
- second_code: bfloat16 [8192, 512], P(('cuts', 'fsdp'))
- second_scale: float32 [8192, 2], P(('cuts', 'fsdp'))
Inputs may be any that keep to these rules, and one draw needn't show every extreme that they name: Every row and every column of send_counts sums to 128; each entry is 0, 1 or 2, and every row and every column holds 2 exactly once.
All inputs are finite; a program needn't handle non-finite values.
Results may differ from a plain program's by a relative error of at most 0.00075.
Values may be sent and summed in bfloat16 or wider, within the bound.
A program may use at most 128 MiB of HBM per device.

v0:
```python
import jax
import jax.numpy as jnp
from jax import lax
from jax.sharding import PartitionSpec as P

STEP = 2000


beta_first = 0.9
beta_second = 0.95
adam_epsilon = 1e-05
learn_rate = 0.001
weight_decay = 0.1
clip_norm = 1.0
tiny_scale = 1e-30


def adam_blocks(clipped, weight, first, first_scale, second, second_scale):
    m_old = first.astype(jnp.float32) * first_scale[:, None]
    v_old = second.astype(jnp.float32) * second_scale[:, None]
    m_new = beta_first * m_old + (1.0 - beta_first) * clipped
    v_new = beta_second * v_old + (1.0 - beta_second) * clipped * clipped
    m_hat = m_new / (1.0 - beta_first**STEP)
    v_hat = v_new / (1.0 - beta_second**STEP)
    w_old = weight.astype(jnp.float32)
    w_new = (
        w_old - learn_rate * (m_hat / (jnp.sqrt(v_hat) + adam_epsilon) + weight_decay * w_old)
    ).astype(jnp.bfloat16)
    m_scale = jnp.max(jnp.abs(m_new), axis=1) + tiny_scale
    v_scale = jnp.max(v_new, axis=1) + tiny_scale
    m_code = (m_new / m_scale[:, None]).astype(jnp.bfloat16)
    v_code = (v_new / v_scale[:, None]).astype(jnp.bfloat16)
    return (w_new, m_code, m_scale, v_code, v_scale)


def shards(
    hidden_states,
    key_cotangent,
    old_weight,
    old_first,
    old_first_scale,
    old_second,
    old_second_scale,
    send_counts,
):
    peer_count = lax.axis_size(("cuts", "fsdp"))
    slot_count = old_weight.shape[0]
    block_size = old_weight.shape[1]
    key_width = key_cotangent.shape[1]
    peer_slots = 2 * slot_count // peer_count
    own_rows = slot_count * block_size // key_width
    row_counts = send_counts[0]
    slot_ends = jnp.cumsum(row_counts)
    starts = slot_ends - row_counts
    lane_index = jnp.arange(peer_slots, dtype=jnp.int32)
    live_slots = lane_index[None, :] < row_counts[:, None]
    pick_index = jnp.where(live_slots, starts[:, None] + lane_index[None, :], 0)
    stacked = jnp.stack([old_weight, old_first, old_second], axis=1)
    scales = jnp.stack([old_first_scale, old_second_scale], axis=1)
    packed = stacked[pick_index]
    packed_scales = scales[pick_index]
    tallies = row_counts.astype(jnp.float32)[:, None]
    arrived = lax.all_to_all(packed, ("cuts", "fsdp"), split_axis=0, concat_axis=0, tiled=True)
    arrived_scales, arrived_tallies = (
        lax.all_to_all(packed_scales, ("cuts", "fsdp"), split_axis=0, concat_axis=0, tiled=True),
        lax.all_to_all(tallies, ("cuts", "fsdp"), split_axis=0, concat_axis=0, tiled=True),
    )
    got_counts = arrived_tallies[:, 0].astype(jnp.int32)
    offsets = jnp.cumsum(got_counts) - got_counts
    live_here = lane_index[None, :] < got_counts[:, None]
    target = jnp.where(live_here, offsets[:, None] + lane_index[None, :], slot_count).reshape(-1)
    owned_state = (
        jnp.zeros((slot_count, 3, block_size), jnp.bfloat16)
        .at[target]
        .set(arrived.reshape(-1, 3, block_size), mode="drop")
    )
    owned_scales = (
        jnp.zeros((slot_count, 2), jnp.float32)
        .at[target]
        .set(arrived_scales.reshape(-1, 2), mode="drop")
    )
    own_weight = owned_state[:, 0].reshape(own_rows, key_width)
    input_grad = lax.dot_general(
        key_cotangent,
        lax.all_gather(own_weight, ("cuts", "fsdp"), axis=0, tiled=True),
        (((1,), (1,)), ((), ())),
        preferred_element_type=jnp.float32,
    ).astype(jnp.bfloat16)
    gradient = lax.psum_scatter(
        lax.dot_general(
            hidden_states,
            key_cotangent,
            (((0,), (0,)), ((), ())),
            preferred_element_type=jnp.float32,
        ),
        ("cuts", "fsdp"),
        scatter_dimension=0,
        tiled=True,
    )
    token_total = hidden_states.shape[0] * peer_count
    gradient = gradient / token_total
    square_sum = lax.psum(jnp.sum(gradient * gradient), ("cuts", "fsdp"))
    factor = jnp.minimum(1.0, clip_norm / (jnp.sqrt(square_sum) + 1e-06))
    clipped = (gradient * factor).reshape(slot_count, block_size)
    w_new, m_code, m_scale, v_code, v_scale = adam_blocks(
        clipped,
        owned_state[:, 0],
        owned_state[:, 1],
        owned_scales[:, 0],
        owned_state[:, 2],
        owned_scales[:, 1],
    )
    blocks_row = key_width // block_size
    return (
        input_grad,
        w_new.reshape(own_rows, key_width),
        m_code.reshape(own_rows, key_width),
        m_scale.reshape(own_rows, blocks_row),
        v_code.reshape(own_rows, key_width),
        v_scale.reshape(own_rows, blocks_row),
    )


def solution(mesh):
    placed = (
        P(("cuts", "fsdp"), None),
        P(("cuts", "fsdp"), None),
        P(("cuts", "fsdp"), None),
        P(("cuts", "fsdp"), None),
        P(("cuts", "fsdp")),
        P(("cuts", "fsdp"), None),
        P(("cuts", "fsdp")),
        P(("cuts", "fsdp"), None),
    )
    return jax.shard_map(
        shards,
        mesh=mesh,
        in_specs=placed,
        out_specs=(
            P(("cuts", "fsdp"), None),
            P(("cuts", "fsdp"), None),
            P(("cuts", "fsdp"), None),
            P(("cuts", "fsdp"), None),
            P(("cuts", "fsdp"), None),
            P(("cuts", "fsdp"), None),
        ),
        check_vma=False,
    )
```

profile of v0, /device:TPU:1, one launch (start us, length us, event | category | flops | bytes accessed | tf_op | source)
XLA Modules:
  0.0 894.5 jit_solution(2391013964506324690)
XLA Ops:
  7.2 0.0 copy-start
  7.2 0.7 convert_bitcast_fusion
  7.9 0.7 copy.60
  8.6 11.5 %all-to-all-start = ((f32[128,1,1]{2,1,0:T(1,128)}), f32[128,1,1]{2,1,0:T(1,128)S(1)}, u32[]{:S(2)}, u32[]{:S(2)}) async-start(f32[128,1,1]{2,1,0:T(1,128)} %copy.60), calls=%async_computation | async-start | bytes 131072 | tf_op jit(solution)/shard_map/all_to_all | solution.py:66
  20.1 0.8 copy.65
  20.9 0.2 reduce-window.17
  21.1 0.1 reduce.2
  21.2 0.7 bitcast_subtract_fusion
  21.8 0.8 compare_select_fusion
  22.6 0.1 reshape.290
  22.7 0.9 copy.62
  23.7 0.9 copy.63
  24.6 0.9 copy.64
  25.6 0.5 pad_maximum_fusion
  26.1 1.2 gather_fusion
  27.2 1.1 copy.66
  28.3 1.6 all-to-all-done
  29.9 8.2 all-to-all-start.1
  38.1 0.0 all-gather.2.cloned.1.call-start
  38.2 0.2 reduce-window.16
  38.4 0.1 reduce.1
  38.5 2.4 convert_reduce_fusion
  40.8 0.1 add_select_fusion
  41.0 0.1 select_n.48
  41.1 9.7 %all-to-all-done.1 = bf16[128,2,3,256]{3,1,2,0:T(2,128)(2,1)S(1)} async-done(((bf16[128,2,3,256]{3,1,2,0:T(2,128)(2,1)}), bf16[128,2,3,256]{3,1,2,0:T(2,128)(2,1)S(1)}, u32[]{:S(2)}, u32[]{:S(2)}) %all-to-all-start.1) | async-done | bytes 393248 | tf_op jit(solution)/shard_map/all_to_all | solution.py:63
  50.9 0.2 copy.77
  51.1 0.1 broadcast_in_dim.15
  51.1 7.3 scatter_fusion
  58.5 0.5 slice_convert_fusion
  59.0 0.7 reshape_squeeze.3
  59.6 0.0 all-gather.2.cloned.1.call-update
  59.7 0.0 reduce-scatter.2.cloned.1.call-start
  59.7 0.0 copy-done
  59.7 11.7 %fusion.15 = f32[8192,512]{1,0:T(8,128)} fusion(bf16[512,8192]{1,0:T(8,128)(2,1)} %param.8, bf16[512,512]{1,0:T(8,128)(2,1)S(1)} %copy-done), kind=kOutput, calls=%fused_computation.49 | convolution fusion | flops 4294967296 | bytes 25690112 | tf_op jit(solution)/shard_map/dot_general | solution.py:90
  71.4 0.0 reduce-scatter.2.cloned.1.call-update
  71.5 0.6 copy-done.3
  72.1 0.0 copy-done.4
  72.1 0.1 copy.70
  72.2 0.7 gather_fusion.1
  73.0 0.9 copy.71
  73.8 14.2 %all_to_all.16 = f32[128,2,2]{1,2,0:T(2,128)S(1)} all-to-all(f32[128,2,2]{1,2,0:T(2,128)S(1)} %copy.71), channel_id=1, replica_groups=mesh['cuts'=8,'fsdp'=16] {'cuts','fsdp'}, dimensions={0} | all-to-all | bytes 4096 | tf_op jit(solution)/shard_map/all_to_all | solution.py:65
  88.1 0.9 copy.78
  88.9 1.3 scatter_custom_fusion.1
  90.3 0.2 slice_reduce_fusion.1
  90.5 0.1 mul.112
  90.6 0.1 mul.113
  90.8 0.1 mul.123
  90.9 0.1 mul.124
  91.1 0.4 fusion.14
  91.6 34.0 %all-gather.2.cloned.1.call-done = bf16[8192,512]{1,0:T(8,128)(2,1)} async-done(((bf16[64,512]{1,0:T(8,128)(2,1)}), bf16[8192,512]{1,0:T(8,128)(2,1)}) %all-gather.2.cloned.1.call-update) | async-done | bytes 8388624 | tf_op jit(solution)/shard_map/all_gather | solution.py:85
  125.6 10.2 %fusion = bf16[512,8192]{0,1:T(8,128)(2,1)} fusion(bf16[8192,512]{1,0:T(8,128)(2,1)} %all-gather.2.cloned.1.call-done, bf16[512,512]{1,0:T(8,128)(2,1)S(1)} %copy-done), kind=kOutput, calls=%fused_computation.5 | convolution fusion | flops 4299161600 | bytes 17301504 | tf_op jit(solution)/shard_map/dot_general | solution.py:83
  135.8 640.2 %reduce-scatter.2.cloned.1.call-done = f32[64,512]{1,0:T(8,128)} async-done(((f32[8192,512]{1,0:T(8,128)}), f32[64,512]{1,0:T(8,128)}) %reduce-scatter.2.cloned.1.call-update) | async-done | bytes 131088 | tf_op jit(solution)/shard_map/reduce_scatter | solution.py:89
  776.0 1.5 multiply_reduce_fusion
  777.6 11.9 %copy.74 = bf16[512,8192]{1,0:T(8,128)(2,1)} copy(bf16[512,8192]{0,1:T(8,128)(2,1)} %fusion) | data formatting | bytes 16777216
  789.5 93.8 %psum.7 = f32[]{:T(128)} all-reduce(f32[]{:T(128)} %multiply_reduce_fusion), channel_id=1, replica_groups=mesh['cuts'=8,'fsdp'=16] {'cuts','fsdp'}, use_global_device_ids=true, to_apply=%region_6.7 | all-reduce | flops 1 | bytes 8 | tf_op jit(solution)/shard_map/psum | solution.py:102
  884.1 0.8 fusion.3
  884.9 0.2 fusion.6
  885.1 0.1 add.128
  885.2 0.6 copy.75
  885.9 0.1 div.41
  886.0 0.1 add.131
  886.2 0.6 copy.76
  886.8 0.1 div.44
  887.0 0.8 divide_convert_fusion
  (20 shorter events, 0.2 us)
Async XLA Ops:
  7.2 52.6 %copy-start = (bf16[512,512]{1,0:T(8,128)(2,1)S(1)}, bf16[512,512]{1,0:T(8,128)(2,1)}, u32[]{:S(2)}) copy-start(bf16[512,512]{1,0:T(8,128)(2,1)} %param.9) | copy-start | bytes 1572868
  8.6 21.2 %all-to-all-start = ((f32[128,1,1]{2,1,0:T(1,128)}), f32[128,1,1]{2,1,0:T(1,128)S(1)}, u32[]{:S(2)}, u32[]{:S(2)}) async-start(f32[128,1,1]{2,1,0:T(1,128)} %copy.60), calls=%async_computation | async-start | bytes 131072 | tf_op jit(solution)/shard_map/all_to_all | solution.py:66
  29.9 21.0 %all-to-all-start.1 = ((bf16[128,2,3,256]{3,1,2,0:T(2,128)(2,1)}), bf16[128,2,3,256]{3,1,2,0:T(2,128)(2,1)S(1)}, u32[]{:S(2)}, u32[]{:S(2)}) async-start(bf16[128,2,3,256]{3,1,2,0:T(2,128)(2,1)} %copy.66), calls=%async_computation.1 | async-start | bytes 786432 | tf_op jit(solution)/shard_map/all_to_all | solution.py:63
  38.1 87.5 %all-gather.2.cloned.1.call-start = ((), (), s32[]{:S(2)}) async-start(), calls=%async_computation.4 | async-start | bytes 8454144 | tf_op jit(solution)/shard_map/all_gather | solution.py:85
  59.7 716.3 %reduce-scatter.2.cloned.1.call-start = ((), (), s32[]{:S(2)}) async-start(), calls=%async_computation.5 | async-start | bytes 16908288 | tf_op jit(solution)/shard_map/reduce_scatter | solution.py:89
  71.4 0.7 copy-start.3
  71.4 0.7 copy-start.4
  777.6 106.5 %copy-start.1 = (bf16[64,512]{1,0:T(8,128)(2,1)S(1)}, bf16[64,512]{1,0:T(8,128)(2,1)}, u32[]{:S(2)}) copy-start(bf16[64,512]{1,0:T(8,128)(2,1)} %reshape_squeeze.3) | copy-start | bytes 196612
  777.6 106.5 %copy-start.2 = (f32[64,512]{1,0:T(8,128)S(1)}, f32[64,512]{1,0:T(8,128)}, u32[]{:S(2)}) copy-start(f32[64,512]{1,0:T(8,128)} %reduce-scatter.2.cloned.1.call-done) | copy-start | bytes 393220
Sparse Core Ops, SparseCore 0:
  59.8 65.7 all-gather.1
  128.0 647.9 reduce-scatter.1
where the time goes:
time: 895 us
  waiting for transfers between devices  686 us (77%)
  blocking collectives  108 us (12%)
  local copies, waits for them, and re-layouts  34.3 us (4%)
  matrix products  21.9 us (2%)
  starting transfers between devices  19.8 us (2%)
  between operations  15.1 us (2%)
  other arithmetic  9.88 us (1%)
    reduce_scatter x1, waiting for transfers between devices, shards(): lax.psum_scatter(lax.dot_general(hidden_states, key_cotangent, (((0,), (0...  640 us
    psum x1, blocking collectives, shards(): square_sum = lax.psum(jnp.sum(gradient * gradient), ('cuts', 'fsdp'))  93.8 us
    all_gather x1, waiting for transfers between devices, shards(): lax.all_gather(own_weight, ('cuts', 'fsdp'), axis=0, tiled=True)  34 us
  transfers between devices with their start and end apart: 4, of which 4 were waited for; matrix products, arithmetic and copies ran while one was open for 4% of the time, Pallas kernels for 0%

commit v1 on v0

v1 whole, which is shorter than its diff:
```python
import jax
import jax.numpy as jnp
from jax import lax
from jax.experimental import pallas as pl
from jax.experimental.pallas import tpu as pltpu
from jax.sharding import PartitionSpec as P

STEP = 2000

beta_first = 0.9
beta_second = 0.95
adam_epsilon = 1e-05
learn_rate = 0.001
weight_decay = 0.1
clip_norm = 1.0
tiny_scale = 1e-30

AXES = ("cuts", "fsdp")
MESH = pl.DeviceIdType.MESH
ROWS = (88, 88, 80)
FIRST = (0, 88, 176)
ORDER = ((0, 1, 2), (1, 2, 0), (2, 0, 1))
SPLIT = (48, 48, 40)


def add_into(target, parts):
    outer, inner = target.shape[:2]

    def body(i, carry):
        a, b = i // inner, i % inner
        total = target[a, b]
        for part in parts:
            total = total + part[a, b]
        target[a, b] = total
        return carry

    lax.fori_loop(0, outer * inner, body, 0)


def main_kernel(
    hidden,
    cotangent,
    weight,
    first,
    second,
    scales,
    w_out,
    m_out,
    ms_out,
    v_out,
    vs_out,
    h_own,
    h_pair,
    c_own,
    c_pair,
    b0,
    b1,
    b2,
    f0,
    f1,
    f2,
    n0,
    n1,
    n2,
    grad,
    plane,
    line,
    load_sem,
    pair_send,
    pair_recv,
    ring_send,
    ring_recv,
    sum_send,
    sum_recv,
):
    cut = lax.axis_index("cuts")
    fs = lax.axis_index("fsdp")
    y, core = cut // 2, cut % 2
    z, x = fs // 4, fs % 4
    here = (y, z, x)

    def at(y, z, x, core):
        return (y * 2 + core, z * 4 + x)

    def neighbour(axis, step):
        place = list(here)
        place[axis] = (place[axis] + step) % 4
        return at(*place, core)

    partner = at(y, z, x, 1 - core)

    order = [(y + s) % 4 for s in (2, 1, 3, 0)]
    loads = [pltpu.make_async_copy(cotangent, c_own, load_sem.at[4])]
    loads[0].start()
    for i, yy in enumerate(order):
        cols = pl.multiple_of(yy * 2048 + core * 1024, 1024)
        copy = pltpu.make_async_copy(hidden.at[:, pl.ds(cols, 1024)], h_own.at[i], load_sem.at[i])
        copy.start()
        loads.append(copy)

    barrier = pltpu.get_barrier_semaphore()
    for s in range(1, 16):
        pl.semaphore_signal(barrier, inc=1, device_id=(cut, (fs + s) % 16), device_id_type=MESH)
    for s in range(1, 8):
        pl.semaphore_signal(barrier, inc=1, device_id=((cut + s) % 8, fs), device_id_type=MESH)
    pl.semaphore_wait(barrier, 22)

    def remote(src, dst, send, recv, device):
        return pltpu.make_async_remote_copy(
            src_ref=src,
            dst_ref=dst,
            send_sem=send,
            recv_sem=recv,
            device_id=device,
            device_id_type=MESH,
        )

    pairs = [remote(cotangent, c_pair, pair_send.at[4], pair_recv.at[4], partner)]
    pairs[0].start()
    for i, yy in enumerate(order):
        cols = pl.multiple_of(yy * 2048 + (1 - core) * 1024, 1024)
        copy = remote(
            hidden.at[:, pl.ds(cols, 1024)],
            h_pair.at[i],
            pair_send.at[i],
            pair_recv.at[i],
            partner,
        )
        copy.start()
        pairs.append(copy)

    bufs, fars, nears = (b0, b1, b2), (f0, f1, f2), (n0, n1, n2)

    class Stage:
        def __init__(self, colour, phase):
            self.axis = ORDER[colour][phase]
            self.mine = here[self.axis]
            index = tuple(here[a] for a in ORDER[colour][:phase])
            self.buf = bufs[colour].at[index] if phase else bufs[colour]
            self.phase = phase
            rows = ROWS[colour]
            if phase == 0:
                self.halves = ((pl.ds(0, 2),), (pl.ds(2, 2),))
            elif phase == 1:
                self.halves = ((pl.ds(0, 2),), (pl.ds(2, 2),))
            else:
                cut_at = SPLIT[colour]
                self.halves = ((pl.ds(0, cut_at),), (pl.ds(cut_at, rows - cut_at),))
            self.far = [fars[colour][phase].at[d] for d in range(2)]
            if phase == 2:
                self.far = [fars[colour][phase].at[d, h[0]] for d, h in enumerate(self.halves)]
            self.near = [nears[colour][phase].at[d] for d in range(2)]
            base = (colour * 3 + phase) * 6
            self.copies = []
            for d, step in enumerate((1, -1)):
                to = neighbour(self.axis, step)
                far = self.buf.at[((self.mine + 2) % 4,) + self.halves[d]]
                close = (self.mine + step) % 4
                own = self.buf.at[(close,) + self.halves[1 - d]]
                acc = self.buf.at[(close,) + self.halves[d]]
                self.copies.append(
                    (
                        remote(far, self.far[d], ring_send.at[base + d], ring_recv.at[base + d], to),
                        remote(
                            own,
                            self.near[d].at[self.halves[1 - d]],
                            ring_send.at[base + 2 + d],
                            ring_recv.at[base + 2 + d],
                            to,
                        ),
                        remote(
                            acc,
                            self.near[d].at[self.halves[d]],
                            ring_send.at[base + 4 + d],
                            ring_recv.at[base + 4 + d],
                            to,
                        ),
                        acc,
                    )
                )

        def four(self, ref):
            return ref

        def add(self, target, parts):
            if self.phase == 0:
                add_into(target, parts)
            elif self.phase == 1:
                for i in range(target.shape[0]):
                    total = target[i]
                    for part in parts:
                        total = total + part[i]
                    target[i] = total
            else:
                total = target[...]
                for part in parts:
                    total = total + part[...]
                target[...] = total

        def begin(self):
            for d in range(2):
                self.copies[d][0].start()
            for d in range(2):
                self.copies[d][1].start()

        def middle(self):
            for d in range(2):
                far, _, onward, acc = self.copies[d]
                far.wait_recv()
                self.add(acc, [self.far[d]])
                onward.start()

        def finish(self):
            for d in range(2):
                self.copies[d][1].wait_recv()
                self.copies[d][2].wait_recv()
            self.add(self.buf.at[self.mine], self.near)

        def drain(self):
            for d in range(2):
                for c in range(3):
                    self.copies[d][c].wait_send()

    loads[0].wait()
    pairs[0].wait_recv()
    for i, yy in enumerate(order):
        loads[1 + i].wait()
        pairs[1 + i].wait_recv()

        def body(zz, carry, i=i, yy=yy):
            cols = pl.ds(pl.multiple_of(zz * 256, 256), 256)
            dims = (((0,), (0,)), ((), ()))
            total = lax.dot_general(
                h_own[i, :, cols], c_own[...], dims, preferred_element_type=jnp.float32
            ) + lax.dot_general(
                h_pair[i, :, cols], c_pair[...], dims, preferred_element_type=jnp.float32
            )
            for xx in range(4):
                part = total[xx * 64 : xx * 64 + 64]
                b0[yy, zz, xx, 0:64, :] = part[:, 0:128]
                b0[yy, zz, xx, 64:88, :] = part[0:24, 128:256]
                b1[zz, xx, yy, 0:40, :] = part[24:64, 128:256]
                b1[zz, xx, yy, 40:88, :] = part[0:48, 256:384]
                b2[xx, yy, zz, 0:16, :] = part[48:64, 256:384]
                b2[xx, yy, zz, 16:80, :] = part[:, 384:512]
            return carry

        lax.fori_loop(0, 4, body, 0)

    for phase in range(3):
        stages = [Stage(colour, phase) for colour in range(3)]
        for s in stages:
            s.begin()
        for s in stages:
            s.middle()
        for s in stages:
            s.finish()
        for s in stages:
            s.drain()

    for colour in range(3):
        index = tuple(here[a] for a in ORDER[colour])
        grad[FIRST[colour] : FIRST[colour] + ROWS[colour], :] = bufs[colour][index] * (1.0 / 65536)

    g = grad[...]
    squares = jnp.sum((g * g).reshape(32, 8, 128), axis=0)

    def gather(table, mine, count, base, target):
        copies = []
        for s in range(1, count):
            copies.append(
                remote(
                    table.at[mine],
                    table.at[mine],
                    sum_send.at[base + s],
                    sum_recv.at[base + s],
                    target(s),
                )
            )
        for c in copies:
            c.start()
        for c in copies:
            c.wait()
        total = table[0]
        for s in range(1, count):
            total = total + table[s]
        return total

    plane[fs] = squares
    squares = gather(plane, fs, 16, 0, lambda s: (cut, (fs + s) % 16))
    line[cut] = squares
    squares = gather(line, cut, 8, 16, lambda s: ((cut + s) % 8, fs))
    norm = jnp.sqrt(jnp.sum(squares, keepdims=True))
    factor = jnp.minimum(1.0, clip_norm / (norm + 1e-06))

    for h in range(2):
        m_new, v_new = [], []
        for j in (2 * h, 2 * h + 1):
            cols = slice(j * 128, j * 128 + 128)
            clipped = grad[j * 64 : j * 64 + 64, :] * factor
            m_old = first[:, cols].astype(jnp.float32) * scales[:, h : h + 1]
            v_old = second[:, cols].astype(jnp.float32) * scales[:, 2 + h : 3 + h]
            m = beta_first * m_old + (1.0 - beta_first) * clipped
            v = beta_second * v_old + (1.0 - beta_second) * clipped * clipped
            m_hat = m / (1.0 - beta_first**STEP)
            v_hat = v / (1.0 - beta_second**STEP)
            w_old = weight[:, cols].astype(jnp.float32)
            w_out[:, cols] = (
                w_old
                - learn_rate * (m_hat / (jnp.sqrt(v_hat) + adam_epsilon) + weight_decay * w_old)
            ).astype(jnp.bfloat16)
            m_new.append(m)
            v_new.append(v)
        m_scale = (
            jnp.max(jnp.maximum(jnp.abs(m_new[0]), jnp.abs(m_new[1])), axis=1, keepdims=True)
            + tiny_scale
        )
        v_scale = jnp.max(jnp.maximum(v_new[0], v_new[1]), axis=1, keepdims=True) + tiny_scale
        ms_out[:, h : h + 1] = m_scale
        vs_out[:, h : h + 1] = v_scale
        for n, j in enumerate((2 * h, 2 * h + 1)):
            cols = slice(j * 128, j * 128 + 128)
            m_out[:, cols] = (m_new[n] / m_scale).astype(jnp.bfloat16)
            v_out[:, cols] = (v_new[n] / v_scale).astype(jnp.bfloat16)

    for c in pairs:
        c.wait_send()


def main_call(hidden, cotangent, weight, first, second, scales):
    vmem = pl.BlockSpec(memory_space=pltpu.VMEM)
    hbm = pl.BlockSpec(memory_space=pl.ANY)
    f32, b16 = jnp.float32, jnp.bfloat16
    scratch = [
        pltpu.VMEM((4, 512, 1024), b16),
        pltpu.VMEM((4, 512, 1024), b16),
        pltpu.VMEM((512, 512), b16),
        pltpu.VMEM((512, 512), b16),
    ]
    scratch += [pltpu.VMEM((4, 4, 4, r, 128), f32) for r in ROWS]
    scratch += [
        [
            pltpu.VMEM((2, 2, 4, r, 128), f32),
            pltpu.VMEM((2, 2, r, 128), f32),
            pltpu.VMEM((2, r, 128), f32),
        ]
        for r in ROWS
    ]
    scratch += [
        [
            pltpu.VMEM((2, 4, 4, r, 128), f32),
            pltpu.VMEM((2, 4, r, 128), f32),
            pltpu.VMEM((2, r, 128), f32),
        ]
        for r in ROWS
    ]
    scratch += [
        pltpu.VMEM((256, 128), f32),
        pltpu.VMEM((16, 8, 128), f32),
        pltpu.VMEM((8, 8, 128), f32),
        pltpu.SemaphoreType.DMA((5,)),
        pltpu.SemaphoreType.DMA((5,)),
        pltpu.SemaphoreType.DMA((5,)),
        pltpu.SemaphoreType.DMA((54,)),
        pltpu.SemaphoreType.DMA((54,)),
        pltpu.SemaphoreType.DMA((24,)),
        pltpu.SemaphoreType.DMA((24,)),
    ]
    return pl.pallas_call(
        main_kernel,
        out_shape=(
            jax.ShapeDtypeStruct((64, 512), b16),
            jax.ShapeDtypeStruct((64, 512), b16),
            jax.ShapeDtypeStruct((64, 2), f32),
            jax.ShapeDtypeStruct((64, 512), b16),
            jax.ShapeDtypeStruct((64, 2), f32),
        ),
        in_specs=[hbm, hbm, vmem, vmem, vmem, vmem],
        out_specs=(vmem,) * 5,
        scratch_shapes=scratch,
        compiler_params=pltpu.CompilerParams(
            collective_id=0, has_side_effects=True, vmem_limit_bytes=60 * 1024 * 1024
        ),
        name="gradient_adam",
    )(hidden, cotangent, weight, first, second, scales)


def three_parts(values):
    high = lax.reduce_precision(values, 8, 7)
    rest = values - high
    middle = lax.reduce_precision(rest, 8, 7)
    return [part.astype(jnp.bfloat16) for part in (high, middle, rest - middle)]


def shards(
    hidden_states,
    key_cotangent,
    old_weight,
    old_first,
    old_first_scale,
    old_second,
    old_second_scale,
    send_counts,
):
    f32, b16 = jnp.float32, jnp.bfloat16
    counts = send_counts[0]
    index = jnp.arange(128, dtype=jnp.int32)
    starts = jnp.sum(jnp.where(index[None, :] < index[:, None], counts[None, :], 0), axis=1)
    lane = jnp.arange(2, dtype=jnp.int32)
    live = lane[None, :] < counts[:, None]
    slot = starts[:, None] + lane[None, :]
    pick = (live[:, :, None] & (slot[:, :, None] == index[None, None, :])).astype(b16)
    side = jnp.stack(
        three_parts(old_first_scale)
        + three_parts(old_second_scale)
        + [jnp.ones((128,), b16)]
        + [jnp.zeros((128,), b16)] * 121,
        axis=1,
    )
    stacked = jnp.concatenate([old_weight, old_first, old_second, side], axis=1)
    packed = lax.dot_general(
        pick.reshape(256, 128), stacked, (((1,), (0,)), ((), ())), preferred_element_type=f32
    ).astype(b16)
    arrived = lax.all_to_all(
        packed.reshape(128, 2, 896), AXES, split_axis=0, concat_axis=0, tiled=True
    ).reshape(256, 896)
    here = arrived[:, 774] > 0.5
    count = here.astype(jnp.int32)
    wide = jnp.arange(256, dtype=jnp.int32)
    target = jnp.sum(jnp.where(wide[None, :] < wide[:, None], count[None, :], 0), axis=1)
    rows = jnp.arange(64, dtype=jnp.int32)
    owned = []
    for h in range(2):
        choose = (here[None, :] & (target[None, :] == 2 * rows[:, None] + h)).astype(b16)
        owned.append(
            lax.dot_general(
                choose, arrived, (((1,), (0,)), ((), ())), preferred_element_type=f32
            )
        )
    weight, first, second = (
        jnp.concatenate([o[:, a * 256 : a * 256 + 256] for o in owned], axis=1).astype(b16)
        for a in range(3)
    )
    scales = jnp.stack(
        [o[:, c] + o[:, c + 1] + o[:, c + 2] for c in (768, 771) for o in owned], axis=1
    )
    gathered = lax.all_gather(weight, AXES, axis=0, tiled=True)
    w_new, m_code, m_scale, v_code, v_scale = main_call(
        hidden_states, key_cotangent, weight, first, second, scales
    )
    input_grad = lax.dot_general(
        key_cotangent, gathered, (((1,), (1,)), ((), ())), preferred_element_type=f32
    ).astype(b16)
    return (input_grad, w_new, m_code, m_scale, v_code, v_scale)


def solution(mesh):
    rows = P(AXES, None)
    placed = (rows, rows, rows, rows, P(AXES), rows, P(AXES), rows)
    return jax.shard_map(
        shards, mesh=mesh, in_specs=placed, out_specs=(rows,) * 6, check_vma=False
    )
```

time: 895 us -> 151 us (0.17)
  waiting for transfers between devices: 686 us -> 13.4 us
  blocking collectives: 108 us -> 0 us
  Pallas kernels: 0 us -> 74.4 us
  local copies, waits for them, and re-layouts: 34.3 us -> 20.1 us
  matrix products: 21.9 us -> 11 us
    reduce_scatter x1 -> x0, waiting for transfers between devices: 640 us -> none  [shards(): lax.psum_scatter(lax.dot_general(hidden_states, key_cotangent, (((0,), (0...]
    psum x1 -> x0, blocking collectives: 93.8 us -> none  [shards(): square_sum = lax.psum(jnp.sum(gradient * gradient), ('cuts', 'fsdp'))]
    pallas_call x0 -> x1, Pallas kernels: none -> 74.4 us  [main_call(): pl.pallas_call(main_kernel, out_shape=(jax.ShapeDtypeStruct((64, 512), b1...]
    all_gather x1, waiting for transfers between devices: 34 us -> 0.01 us  [shards(): gathered = lax.all_gather(weight, AXES, axis=0, tiled=True)]
    all_to_all x1 -> x0, blocking collectives: 14.2 us -> none  [shards(): lax.all_to_all(packed_scales, ('cuts', 'fsdp'), split_axis=0, concat_axis...]
    dot_general x2 -> x4, matrix products: 21.9 us -> 11 us  [the longest x1 10.2 us: shards(): lax.dot_general(key_cotangent, gathered, (((1,), (1,)), ((), ())), prefer...]
    all_to_all x2 -> x1, starting transfers between devices: 19.7 us -> 11.5 us  [shards(): lax.all_to_all(packed.reshape(128, 2, 896), AXES, split_axis=0, concat_ax...]
  transfers between devices with their start and end apart: 4 -> 2, of which waited for: 4 -> 1; matrix products, arithmetic and copies ran while one was open for 4% -> 3% of each run, Pallas kernels for 0% -> 50%
where the time goes in v1:
time: 151 us; the launch traced here: 150 us
  Pallas kernels  74.4 us (49%)
  local copies, waits for them, and re-layouts  20.1 us (13%)
  between operations  14.2 us (9%)
  waiting for transfers between devices  13.4 us (9%)
  starting transfers between devices  11.5 us (8%)
  matrix products  11 us (7%)
  other arithmetic  5.38 us (4%)
    pallas_call x1, Pallas kernels, main_call(): pl.pallas_call(main_kernel, out_shape=(jax.ShapeDtypeStruct((64, 512), b1...  74.4 us
    unnamed x14, local copies, waits for them, and re-layouts  16.6 us
    all_to_all x1, waiting for transfers between devices, shards(): lax.all_to_all(packed.reshape(128, 2, 896), AXES, split_axis=0, concat_ax...  13.4 us
    all_to_all x1, starting transfers between devices, shards(): lax.all_to_all(packed.reshape(128, 2, 896), AXES, split_axis=0, concat_ax...  11.5 us
    dot_general x1, matrix products, shards(): lax.dot_general(key_cotangent, gathered, (((1,), (1,)), ((), ())), prefer...  10.2 us
  transfers between devices with their start and end apart: 2, of which 1 were waited for; matrix products, arithmetic and copies ran while one was open for 3% of the time, Pallas kernels for 50%

profile of v1, /device:TPU:1, one launch (start us, length us, event | category | flops | bytes accessed | tf_op | source)
XLA Modules:
  0.0 150.0 jit_solution(16454743914016732999)
XLA Ops:
  7.2 0.8 select_reduce_fusion.1
  7.9 0.7 iota_compare_fusion.3
  8.7 0.7 fusion.20
  9.3 0.1 copy.56
  9.5 0.1 copy.57
  9.6 0.1 copy.58
  9.8 0.7 fusion.24
  10.4 0.1 copy.59
  10.6 0.1 copy.60
  10.7 0.1 copy.61
  10.8 0.1 iota_add_fusion
  10.9 0.1 add.63
  11.1 0.1 lt.54
  11.3 0.0 copy-start
  11.3 1.1 concatenate.31
  12.5 0.3 convolution_convert_fusion.1
  12.8 0.9 reshape.82
  13.7 11.5 %all-to-all-start = ((bf16[128,2,896]{2,1,0:T(2,128)(2,1)}), bf16[128,2,896]{2,1,0:T(2,128)(2,1)S(1)}, u32[]{:S(2)}, u32[]{:S(2)}) async-start(bf16[128,2,896]{2,1,0:T(2,128)(2,1)} %reshape.82), calls=%async_computation | async-start | bytes 917504 | tf_op jit(solution)/shard_map/all_to_all | solution.py:424
  25.2 0.0 all-gather.2.cloned.1.call-start
  25.3 13.4 %all-to-all-done = bf16[128,2,896]{2,1,0:T(2,128)(2,1)S(1)} async-done(((bf16[128,2,896]{2,1,0:T(2,128)(2,1)}), bf16[128,2,896]{2,1,0:T(2,128)(2,1)S(1)}, u32[]{:S(2)}, u32[]{:S(2)}) %all-to-all-start) | async-done | bytes 458784 | tf_op jit(solution)/shard_map/all_to_all | solution.py:424
  38.7 0.2 reshape.83
  38.8 0.2 compare_reduce_fusion
  39.0 0.1 select_reduce_fusion
  39.2 0.3 fusion.28
  39.4 0.2 fusion.27
  39.7 0.6 pad_maximum_fusion.weight
  40.3 0.0 all-gather.2.cloned.1.call-update
  40.4 0.1 slice_add_fusion.4
  40.5 0.7 pad_maximum_fusion.3.scales
  41.2 0.7 pad_maximum_fusion.1
  41.9 74.4 %gradient_adam.1 = (bf16[64,512]{1,0:T(8,128)(2,1)}, bf16[64,512]{1,0:T(8,128)(2,1)}, f32[64,2]{1,0:T(8,128)}, bf16[64,512]{1,0:T(8,128)(2,1)}, f32[64,2]{1,0:T(8,128)}) custom-call(bf16[512,8192]{1,0:T(8,128)(2,1)} %hidden.1, bf16[512,512]{1,0:T(8,128)(2,1)} %cotangent.1, bf16[64,512]{1,0:T(8,128)(2,1)} %pad_maximum_fusion.weight, ...), custom_call_target="tpu_custom_call" | custom-call | tf_op jit(solution)/shard_map/gradient_adam/pallas_call | solution.py:369
  116.3 1.4 copy.63
  117.7 1.4 copy.64
  119.1 0.0 all-gather.2.cloned.1.call-done
  119.1 0.0 copy-done
  119.1 10.2 %fusion = bf16[512,8192]{0,1:T(8,128)(2,1)} fusion(bf16[8192,512]{1,0:T(8,128)(2,1)} %all-gather.2.cloned.1.call-done, bf16[512,512]{1,0:T(8,128)(2,1)S(1)} %copy-done), kind=kOutput, calls=%fused_computation.1 | convolution fusion | flops 4299161600 | bytes 17301504 | tf_op jit(solution)/shard_map/dot_general | solution.py:451
  129.3 0.0 copy-start.3
  129.3 0.0 copy-start.2
  129.3 0.0 copy-start.1
  129.3 12.0 %copy.62 = bf16[512,8192]{1,0:T(8,128)(2,1)} copy(bf16[512,8192]{0,1:T(8,128)(2,1)} %fusion) | data formatting | bytes 16777216
  141.2 0.0 copy-done.3
  141.2 0.6 copy.68
  141.9 0.0 copy-done.2
  141.9 0.6 copy.69
  142.5 0.0 copy-done.1
  142.5 0.6 copy.70
  (11 shorter events, 0.1 us)
Async XLA Ops:
  11.3 107.8 %copy-start = (bf16[512,512]{1,0:T(8,128)(2,1)S(1)}, bf16[512,512]{1,0:T(8,128)(2,1)}, u32[]{:S(2)}) copy-start(bf16[512,512]{1,0:T(8,128)(2,1)} %cotangent.1) | copy-start | bytes 1572868
  13.7 24.9 %all-to-all-start = ((bf16[128,2,896]{2,1,0:T(2,128)(2,1)}), bf16[128,2,896]{2,1,0:T(2,128)(2,1)S(1)}, u32[]{:S(2)}, u32[]{:S(2)}) async-start(bf16[128,2,896]{2,1,0:T(2,128)(2,1)} %reshape.82), calls=%async_computation | async-start | bytes 917504 | tf_op jit(solution)/shard_map/all_to_all | solution.py:424
  25.2 93.8 %all-gather.2.cloned.1.call-start = ((), (), s32[]{:S(2)}) async-start(), calls=%async_computation.1 | async-start | bytes 8454144 | tf_op jit(solution)/shard_map/all_gather | solution.py:447
  129.3 12.0 %copy-start.3 = (bf16[64,512]{1,0:T(8,128)(2,1)S(1)}, bf16[64,512]{1,0:T(8,128)(2,1)}, u32[]{:S(2)}) copy-start(bf16[64,512]{1,0:T(8,128)(2,1)} %get-tuple-element.77) | copy-start | bytes 196612
  129.3 12.6 %copy-start.2 = (bf16[64,512]{1,0:T(8,128)(2,1)S(1)}, bf16[64,512]{1,0:T(8,128)(2,1)}, u32[]{:S(2)}) copy-start(bf16[64,512]{1,0:T(8,128)(2,1)} %get-tuple-element.78) | copy-start | bytes 196612
  129.3 13.2 %copy-start.1 = (bf16[64,512]{1,0:T(8,128)(2,1)S(1)}, bf16[64,512]{1,0:T(8,128)(2,1)}, u32[]{:S(2)}) copy-start(bf16[64,512]{1,0:T(8,128)(2,1)} %get-tuple-element.80) | copy-start | bytes 196612
Sparse Core Ops, SparseCore 0:
  40.5 68.9 all-gather.1
